TPU v7x, 512 devices: a whole 4x4x16 slice. The times are simulated.
512 devices in a mesh: ctx: 64 (over z_hi, x, y), exp: 8 (over z_lo, core).
Axes of the slice: x: 4, y: 4, z: 16 (z_hi: 4, z_lo: 4; z = z_hi * 4 + z_lo), core: 2. Of those that a mesh axis runs over, the one named last changes fastest.
Arguments:
- queries: bfloat16 [65536, 2048], P('ctx', 'exp'), may hold values from -150 to 150
- keys: bfloat16 [65536, 2048], P('ctx', 'exp'), may hold values from -6 to 6
- values: bfloat16 [65536, 2048], P('ctx', 'exp'), may hold values from -6 to 6
- segment_ids: int32 [65536], P('ctx'), may hold values from 0 to 255, never falling along the last dimension, each value on 1 to 1024 neighbouring positions
- out_proj: bfloat16 [2048, 1280], P('exp'), may hold values from -0.125 to 0.125
- residual: bfloat16 [65536, 1280], P(('ctx', 'exp')), may hold values from -6 to 6
- norm_gain: float32 [1280], replicated, may hold values from 0.1 to 1.9
- expert_ids: int32 [65536, 6], P(('ctx', 'exp')), may hold values from 0 to 63, all different within a row; in each aligned block of 128 rows (0 to 127, 128 to 255, ...) at most 16 rows name the same one
- gate_weights: float32 [65536, 6], P(('ctx', 'exp')), may hold values from 0.05 to 0.4
- expert_up: bfloat16 [64, 768, 1280], P('ctx', 'exp'), may hold values from -0.15625 to 0.15625
- expert_down: bfloat16 [64, 768, 1280], P('ctx', 'exp'), may hold values from -0.21875 to 0.21875
Outputs:
- layer_out: bfloat16 [65536, 1280], P(('ctx', 'exp'))
Inputs may be any that keep to these rules, and one draw needn't show every extreme that they name: `segment_ids`: segment ids never fall; every segment spans 1 to 1024 consecutive tokens, one exactly 1024. `expert_ids`: each row names 6 different experts. In each aligned block of 128 rows (the rows of one device) no expert is named by more than 16 rows, a bound that some block reaches.
All inputs are finite; a program needn't handle non-finite values.
Results may differ from a plain program's by a relative error of at most 0.01.
Values may be sent and summed in bfloat16 or wider, within the bound.
A program may use at most 64 MiB of HBM per device.

v0:
```python
import jax
import jax.numpy as jnp
from jax import lax
from jax.sharding import PartitionSpec as P

HEAD = 128
TOP = 6


def shifted(block, axis, distance):
    devices = range(lax.axis_size(axis))
    route = [(i - distance, i) for i in devices if i - distance in devices]
    return lax.ppermute(block, axis, route)


def block_attention(query_rows, key_rows, value_rows, allowed):
    scores = jnp.dot(query_rows, key_rows.T, preferred_element_type=jnp.float32) * HEAD ** (-0.5)
    row_max = jnp.max(jnp.where(allowed, scores, -1e30), axis=1, keepdims=True)
    weights = jnp.exp(jnp.where(allowed, scores - row_max, -jnp.inf))
    probabilities = (weights / jnp.sum(weights, axis=1, keepdims=True)).astype(jnp.bfloat16)
    return jnp.dot(probabilities, value_rows, preferred_element_type=jnp.float32).astype(
        jnp.bfloat16
    )


def shards(
    queries,
    keys,
    values,
    segment_ids,
    out_proj,
    residual,
    norm_gain,
    expert_ids,
    gate_weights,
    expert_up,
    expert_down,
):
    up_whole, down_whole = (
        lax.all_gather(expert_up, "exp", axis=1, tiled=True),
        lax.all_gather(expert_down, "exp", axis=1, tiled=True),
    )
    shard_len = queries.shape[0]
    heads_here = queries.shape[1] // HEAD
    block_rows = min(512, shard_len)
    blocks = shard_len // block_rows
    seg_marks = segment_ids + 1
    early_keys, early_values, early_marks = shifted((keys, values, seg_marks), "ctx", 1)
    positions = jnp.arange(shard_len, dtype=jnp.int32)
    both_marks = jnp.concatenate([early_marks, seg_marks])
    both_positions = jnp.concatenate([positions - shard_len, positions])
    head_outputs = []
    for head_index in range(heads_here):
        low = head_index * HEAD
        query_head = queries[:, low : low + HEAD]
        key_head = keys[:, low : low + HEAD]
        value_head = values[:, low : low + HEAD]
        both_keys = jnp.concatenate([early_keys[:, low : low + HEAD], key_head], axis=0)
        both_values = jnp.concatenate([early_values[:, low : low + HEAD], value_head], axis=0)

        def one_block(block_index):
            start_row = block_index * block_rows
            query_rows = lax.dynamic_slice_in_dim(query_head, start_row, block_rows, 0)
            query_marks = lax.dynamic_slice_in_dim(seg_marks, start_row, block_rows, 0)
            query_positions = start_row + jnp.arange(block_rows, dtype=jnp.int32)
            allowed = (both_marks[None, :] == query_marks[:, None]) & (
                both_positions[None, :] <= query_positions[:, None]
            )
            return block_attention(query_rows, both_keys, both_values, allowed)

        block_outputs = lax.map(one_block, jnp.arange(blocks, dtype=jnp.int32))
        head_outputs.append(block_outputs.reshape(shard_len, HEAD))
    attention = jnp.concatenate(head_outputs, axis=1)
    row_block = attention
    projected = lax.psum_scatter(
        jnp.dot(row_block, out_proj, preferred_element_type=jnp.float32).astype(jnp.bfloat16),
        "exp",
        scatter_dimension=0,
        tiled=True,
    ).astype(jnp.float32)
    stream = (residual.astype(jnp.float32) + projected).astype(jnp.bfloat16)
    stream_f = stream.astype(jnp.float32)
    mean_square = jnp.mean(stream_f * stream_f, axis=1, keepdims=True)
    normed = (stream_f * lax.rsqrt(mean_square + 1e-06) * norm_gain[None, :]).astype(jnp.bfloat16)
    tok_rows = stream.shape[0]
    feature_count = stream.shape[1]
    experts = lax.axis_size("ctx")
    slot_count = max(2, tok_rows * TOP * 4 // (3 * experts))
    flat_ids = expert_ids.reshape(-1)
    one_hot = (flat_ids[:, None] == jnp.arange(experts, dtype=jnp.int32)[None, :]).astype(jnp.int32)
    earlier = jnp.cumsum(one_hot, axis=0) - one_hot
    slot_rank = jnp.sum(earlier * one_hot, axis=1)
    slot_index = flat_ids * slot_count + slot_rank
    slot_grid = slot_index.reshape(tok_rows, TOP)
    placing = jnp.any(
        slot_grid[None, :, :] == jnp.arange(experts * slot_count, dtype=jnp.int32)[:, None, None],
        axis=2,
    )
    outgoing = jnp.dot(
        placing.astype(jnp.bfloat16), normed, preferred_element_type=jnp.float32
    ).astype(jnp.bfloat16)
    outgoing = outgoing.reshape(experts, slot_count, feature_count)
    arrived = lax.all_to_all(outgoing, "ctx", split_axis=0, concat_axis=0, tiled=True)
    sources, item_count, width_here = arrived.shape
    row_block = arrived.reshape(sources * item_count, width_here)
    hidden = jax.nn.silu(
        jnp.dot(row_block, up_whole[0].T, preferred_element_type=jnp.float32)
    ).astype(jnp.bfloat16)
    result = jnp.dot(hidden, down_whole[0], preferred_element_type=jnp.float32).astype(jnp.bfloat16)
    result = result.reshape(sources, item_count, width_here)
    returned = lax.all_to_all(result, "ctx", split_axis=0, concat_axis=0, tiled=True)
    returned_flat = returned.reshape(experts * slot_count, feature_count)
    picked = returned_flat[slot_index].reshape(tok_rows, TOP, feature_count).astype(jnp.float32)
    mixture = jnp.sum(gate_weights[:, :, None] * picked, axis=1)
    return (stream_f + mixture).astype(jnp.bfloat16)


def solution(mesh):
    in_specs = (
        P("ctx", "exp"),
        P("ctx", "exp"),
        P("ctx", "exp"),
        P("ctx"),
        P("exp", None),
        P(("ctx", "exp"), None),
        P(),
        P(("ctx", "exp"), None),
        P(("ctx", "exp"), None),
        P("ctx", "exp", None),
        P("ctx", "exp", None),
    )
    out_specs = P(("ctx", "exp"), None)
    return jax.shard_map(shards, mesh=mesh, in_specs=in_specs, out_specs=out_specs, check_vma=False)
```

profile of v0, /device:TPU:8, one launch (start us, length us, event | category | flops | bytes accessed | tf_op | source)
XLA Modules:
  0.0 555.8 jit_solution(545644793723613808)
XLA Ops:
  7.3 3.5 collective-permute-start
  10.8 3.2 collective-permute-start.1
  14.0 3.1 collective-permute-start.2
  19.2 1.8 fusion.50
  21.0 7.7 %collective-permute-done.1 = bf16[1024,256]{1,0:T(8,128)(2,1)S(1)} collective-permute-done((bf16[1024,256]{1,0:T(8,128)(2,1)}, bf16[1024,256]{1,0:T(8,128)(2,1)S(1)}, u32[]{:S(2)}, u32[]{:S(2)}) %collective-permute-start.1) | collective-permute-done | bytes 524320 | tf_op jit(solution)/shard_map/ppermute | solution.py:13
  28.8 8.8 %collective-permute-done.2 = bf16[1024,256]{1,0:T(8,128)(2,1)S(1)} collective-permute-done((bf16[1024,256]{1,0:T(8,128)(2,1)}, bf16[1024,256]{1,0:T(8,128)(2,1)S(1)}, u32[]{:S(2)}, u32[]{:S(2)}) %collective-permute-start.2) | collective-permute-done | bytes 524320 | tf_op jit(solution)/shard_map/ppermute | solution.py:13
  38.5 15.9 %while.20 = (s32[]{:T(128)}, bf16[2,512,128]{2,1,0:T(8,128)(2,1)S(1)}, s32[2048]{0:T(1024)S(1)}, s32[2]{0:T(128)S(1)}, s32[1024]{0:T(1024)}, /*index=5*/s32[2048...) while((s32[]{:T(128)}, ...), condition=%wide.region_3.4_spmd, body=%wide.region_0.3_spmd.sunk | while | flops 558956032 | bytes 16068835 | solution.py:71
  40.5 2.2 select_reduce_fusion.4
  42.7 1.7 fusion.68
  44.5 2.0 fusion.69
  48.4 2.2 select_reduce_fusion.4
  50.7 1.7 fusion.68
  52.4 2.0 fusion.69
  54.4 13.9 %while.21 = (s32[]{:T(128)}, bf16[2,512,128]{2,1,0:T(8,128)(2,1)S(1)}, s32[2048]{0:T(1024)S(1)}, s32[2]{0:T(128)S(1)}, s32[1024]{0:T(1024)}, /*index=5*/s32[2048...) while((s32[]{:T(128)}, ...), condition=%wide.region_7.8_spmd, body=%wide.region_4.7_spmd.sunk | while | flops 558956032 | bytes 13971655 | solution.py:71
  57.7 1.7 fusion.72
  59.4 2.0 fusion.73
  63.4 1.3 select_reduce_fusion.5
  64.7 1.7 fusion.72
  66.4 2.0 fusion.73
  68.4 2.4 convolution_convert_fusion.2
  71.2 1.8 reduce-window.6
  74.2 119.5 %reduce-scatter.2.cloned.1.call-done = bf16[128,1280]{1,0:T(8,128)(2,1)} async-done(((bf16[1024,1280]{1,0:T(8,128)(2,1)}), bf16[128,1280]{1,0:T(8,128)(2,1)}) %reduce-scatter.2.cloned.1.call-update) | async-done | bytes 327696 | tf_op jit(solution)/shard_map/reduce_scatter | solution.py:75
  194.9 3.4 convolution_convert_fusion.1
  198.3 16.5 %all-to-all-start = ((bf16[64,16,1280]{2,1,0:T(8,128)(2,1)}), bf16[64,16,1280]{2,1,0:T(8,128)(2,1)S(1)}, u32[]{:S(2)}, u32[]{:S(2)}) async-start(bf16[64,16,1280]{2,1,0:T(8,128)(2,1)} %bitcast.7), calls=%async_computation.1 | async-start | bytes 5242880 | tf_op jit(solution)/shard_map/all_to_all | solution.py:103
  216.3 118.3 %all-gather.3.cloned.1.call-done = bf16[1,768,1280]{2,1,0:T(8,128)(2,1)} async-done(((bf16[1,96,1280]{2,1,0:T(8,128)(2,1)}), bf16[1,768,1280]{2,1,0:T(8,128)(2,1)}) %all-gather.3.cloned.1.call-update) | async-done | bytes 1966096 | tf_op jit(solution)/shard_map/all_gather | solution.py:40
  334.5 54.7 %all-gather.5.cloned.1.call-done = bf16[1,768,1280]{2,1,0:T(8,128)(2,1)} async-done(((bf16[1,96,1280]{2,1,0:T(8,128)(2,1)}), bf16[1,768,1280]{2,1,0:T(8,128)(2,1)}) %all-gather.5.cloned.1.call-update) | async-done | bytes 1966096 | tf_op jit(solution)/shard_map/all_gather | solution.py:41
  389.3 8.0 %convolution_convert_fusion = bf16[1024,1280]{1,0:T(8,128)(2,1)} fusion(bf16[1,768,1280]{2,1,0:T(8,128)(2,1)} %all-gather.5.cloned.1.call-done, bf16[1024,1280]{1,0:T(8,128)(2,1)S(1)} %bitcast.70, bf16[1,768,1280]{2,1,0:T(8,128)(2,1)} %all-gather.3.cloned.1.call-done), kind=kOutput, calls=%fused_computation.32 | convolution fusion | flops 4031774720 | bytes 9175040 | tf_op jit(solution)/shard_map/dot_general | solution.py:109
  397.3 16.4 %all-to-all-start.1 = ((bf16[64,16,1280]{2,1,0:T(8,128)(2,1)}), bf16[64,16,1280]{2,1,0:T(8,128)(2,1)S(1)}, u32[]{:S(2)}, u32[]{:S(2)}) async-start(bf16[64,16,1280]{2,1,0:T(8,128)(2,1)} %bitcast.71), calls=%async_computation.2 | async-start | bytes 5242880 | tf_op jit(solution)/shard_map/all_to_all | solution.py:111
  414.0 122.0 %all-to-all-done.1 = bf16[64,16,1280]{2,1,0:T(8,128)(2,1)S(1)} async-done(((bf16[64,16,1280]{2,1,0:T(8,128)(2,1)}), bf16[64,16,1280]{2,1,0:T(8,128)(2,1)S(1)}, u32[]{:S(2)}, u32[]{:S(2)}) %all-to-all-start.1) | async-done | bytes 2621472 | tf_op jit(solution)/shard_map/all_to_all | solution.py:111
  536.0 3.7 gather_fusion
  539.7 4.5 reshape.112
  544.2 4.2 multiply_reduce_fusion
  (74 shorter events, 16.1 us)
Async XLA Ops:
  6.5 61.9 %copy-start = (bf16[256,1280]{1,0:T(8,128)(2,1)S(1)}, bf16[256,1280]{1,0:T(8,128)(2,1)}, u32[]{:S(2)}) copy-start(bf16[256,1280]{1,0:T(8,128)(2,1)} %param.19) | copy-start | bytes 1966084
  6.5 187.2 %reduce-scatter.2.cloned.1.call-start = ((), (), s32[]{:S(2)}) async-start(), calls=%async_computation.3 | async-start | bytes 2949120 | tf_op jit(solution)/shard_map/reduce_scatter | solution.py:75
  7.3 21.4 %copy-start.5 = (s32[1024]{0:T(1024)}, s32[1024]{0:T(1024)S(1)}, u32[]{:S(2)}) copy-start(s32[1024]{0:T(1024)S(1)} %broadcast_add_fusion) | copy-start | bytes 12292
  7.3 13.7 %collective-permute-start = (s32[1024]{0:T(1024)S(1)}, s32[1024]{0:T(1024)S(1)}, u32[]{:S(2)}, u32[]{:S(2)}) collective-permute-start(s32[1024]{0:T(1024)S(1)} %broadcast_add_fusion), channel_id=1, source_target_pairs={{0,8},{8,16},{16,24},{24,32},{32,40},{40,48},{48,56},{56,64},{64,7... | collective-permute-start | bytes 12296 | tf_op jit(solution)/shard_map/ppermute | solution.py:13
  10.8 17.9 %collective-permute-start.1 = (bf16[1024,256]{1,0:T(8,128)(2,1)}, bf16[1024,256]{1,0:T(8,128)(2,1)S(1)}, u32[]{:S(2)}, u32[]{:S(2)}) collective-permute-start(bf16[1024,256]{1,0:T(8,128)(2,1)} %param.16), channel_id=1, source_target_pairs={{0,8},{8,16},{16,24},{24,32},{32,40},{40,48},{48,56},{56,64},{64,7... | collective-permute-start | bytes 1572872 | tf_op jit(solution)/shard_map/ppermute | solution.py:13
  14.0 23.6 %collective-permute-start.2 = (bf16[1024,256]{1,0:T(8,128)(2,1)}, bf16[1024,256]{1,0:T(8,128)(2,1)S(1)}, u32[]{:S(2)}, u32[]{:S(2)}) collective-permute-start(bf16[1024,256]{1,0:T(8,128)(2,1)} %param.17), channel_id=1, source_target_pairs={{0,8},{8,16},{16,24},{24,32},{32,40},{40,48},{48,56},{56,64},{64,7... | collective-permute-start | bytes 1572872 | tf_op jit(solution)/shard_map/ppermute | solution.py:13
  40.5 3.9 copy-start.4
  48.4 3.9 copy-start.4
  68.4 2.4 copy-start.7
  68.4 125.3 %copy-start.1 = (bf16[128,1280]{1,0:T(8,128)(2,1)S(1)}, bf16[128,1280]{1,0:T(8,128)(2,1)}, u32[]{:S(2)}) copy-start(bf16[128,1280]{1,0:T(8,128)(2,1)} %param.20) | copy-start | bytes 983044
  68.4 126.5 %copy-start.6 = (f32[1280]{0:T(1024)S(1)}, f32[1280]{0:T(1024)}, u32[]{:S(2)}) copy-start(f32[1280]{0:T(1024)} %param.21) | copy-start | bytes 15364
  198.3 190.9 %all-to-all-start = ((bf16[64,16,1280]{2,1,0:T(8,128)(2,1)}), bf16[64,16,1280]{2,1,0:T(8,128)(2,1)S(1)}, u32[]{:S(2)}, u32[]{:S(2)}) async-start(bf16[64,16,1280]{2,1,0:T(8,128)(2,1)} %bitcast.7), calls=%async_computation.1 | async-start | bytes 5242880 | tf_op jit(solution)/shard_map/all_to_all | solution.py:103
  214.8 119.7 %all-gather.3.cloned.1.call-start = ((), (), s32[]{:S(2)}) async-start(), calls=%async_computation.4 | async-start | bytes 2211840 | tf_op jit(solution)/shard_map/all_gather | solution.py:40
  215.5 173.7 %all-gather.5.cloned.1.call-start = ((), (), s32[]{:S(2)}) async-start(), calls=%async_computation.5 | async-start | bytes 2211840 | tf_op jit(solution)/shard_map/all_gather | solution.py:41
  397.3 16.5 %copy-start.8 = (f32[128,6]{0,1:T(8,128)S(1)}, f32[128,6]{0,1:T(8,128)}, u32[]{:S(2)}) copy-start(f32[128,6]{0,1:T(8,128)} %param.23) | copy-start | bytes 9220
  397.3 138.7 %all-to-all-start.1 = ((bf16[64,16,1280]{2,1,0:T(8,128)(2,1)}), bf16[64,16,1280]{2,1,0:T(8,128)(2,1)S(1)}, u32[]{:S(2)}, u32[]{:S(2)}) async-start(bf16[64,16,1280]{2,1,0:T(8,128)(2,1)} %bitcast.71), calls=%async_computation.2 | async-start | bytes 5242880 | tf_op jit(solution)/shard_map/all_to_all | solution.py:111
  544.2 4.2 copy-start.2
  544.2 4.2 copy-start.3
Sparse Core Ops, SparseCore 0:
  70.9 122.7 reduce-scatter.1
  217.7 116.8 all-gather.2
  336.6 52.5 all-gather.4
where the time goes:
time: 557 us; the launch traced here: 556 us
  waiting for transfers between devices  432 us (78%)
  starting transfers between devices  42.8 us (8%)
  matrix products  28.7 us (5%)
  local copies, waits for them, and re-layouts  18.8 us (3%)
  other arithmetic  17.2 us (3%)
  between operations  13.4 us (2%)
    all_to_all x1, waiting for transfers between devices, shards(): lax.all_to_all(result, 'ctx', split_axis=0, concat_axis=0, tiled=True)  122 us
    reduce_scatter x1, waiting for transfers between devices, shards(): lax.psum_scatter(jnp.dot(row_block, out_proj, preferred_element_type=jnp....  120 us
    all_gather x1, waiting for transfers between devices, shards(): lax.all_gather(expert_up, 'exp', axis=1, tiled=True)  118 us
    all_gather x1, waiting for transfers between devices, shards(): lax.all_gather(expert_down, 'exp', axis=1, tiled=True)  54.7 us
    all_to_all x1, starting transfers between devices, shards(): lax.all_to_all(outgoing, 'ctx', split_axis=0, concat_axis=0, tiled=True)  16.5 us
    ppermute x3, waiting for transfers between devices, shifted(): return lax.ppermute(block, axis, route)  16.4 us
    all_to_all x1, starting transfers between devices, shards(): lax.all_to_all(result, 'ctx', split_axis=0, concat_axis=0, tiled=True)  16.4 us
  transfers between devices with their start and end apart: 8, of which 6 were waited for; matrix products, arithmetic and copies ran while one was open for 1% of the time, Pallas kernels for 0%

commit v1 on v0

--- a/solution.py
+++ b/solution.py
@@ -37,7 +37,9 @@
     expert_down,
 ):
     up_whole, down_whole = (
-        lax.all_gather(expert_up, "exp", axis=1, tiled=True),
+        jnp.concatenate(
+            lax.all_to_all(jnp.stack([expert_up] * lax.axis_size("exp")), "exp", 0, 0), axis=1
+        ),
         lax.all_gather(expert_down, "exp", axis=1, tiled=True),
     )
     shard_len = queries.shape[0]

time: 557 us -> 516 us (0.926)
  the two profiles are of different devices: /device:TPU:8 before, /device:TPU:40 now
where the time goes in v1:
time: 516 us; the launch traced here: 515 us
  waiting for transfers between devices  378 us (73%)
  starting transfers between devices  47.1 us (9%)
  matrix products  31.3 us (6%)
  local copies, waits for them, and re-layouts  22.5 us (4%)
  other arithmetic  19.4 us (4%)
  between operations  13.7 us (3%)
    all_to_all x1, waiting for transfers between devices, shards(): lax.all_to_all(result, 'ctx', split_axis=0, concat_axis=0, tiled=True)  124 us
    reduce_scatter x1, waiting for transfers between devices, shards(): lax.psum_scatter(jnp.dot(row_block, out_proj, preferred_element_type=jnp....  117 us
    all_gather x1, waiting for transfers between devices, shards(): lax.all_gather(expert_down, 'exp', axis=1, tiled=True)  113 us
    all_to_all x1, waiting for transfers between devices, shards(): lax.all_to_all(outgoing, 'ctx', split_axis=0, concat_axis=0, tiled=True)  19.3 us
    all_to_all x1, starting transfers between devices, shards(): lax.all_to_all(outgoing, 'ctx', split_axis=0, concat_axis=0, tiled=True)  16.2 us
    all_to_all x1, starting transfers between devices, shards(): lax.all_to_all(result, 'ctx', split_axis=0, concat_axis=0, tiled=True)  14.9 us
  transfers between devices with their start and end apart: 8, of which 5 were waited for; matrix products, arithmetic and copies ran while one was open for 10% of the time, Pallas kernels for 0%

profile of v1, /device:TPU:40, one launch (start us, length us, event | category | flops | bytes accessed | tf_op | source)
XLA Modules:
  0.0 514.9 jit_solution(414561323530542581)
XLA Ops:
  7.3 3.5 collective-permute-start
  10.8 3.2 collective-permute-start.1
  14.0 3.1 collective-permute-start.2
  17.0 2.3 stack.2
  19.4 6.0 %all-to-all-start.1 = ((bf16[8,1,96,1280]{3,2,1,0:T(8,128)(2,1)}), bf16[8,1,96,1280]{3,2,1,0:T(8,128)(2,1)S(1)}, u32[]{:S(2)}, u32[]{:S(2)}) async-start(bf16[8,1,96,1280]{3,2,1,0:T(8,128)(2,1)} %stack.2), calls=%async_computation.2 | async-start | bytes 3932160 | tf_op jit(solution)/shard_map/all_to_all | solution.py:41
  25.4 1.8 fusion.44
  28.2 1.9 fusion.45
  31.2 2.0 pad_maximum_fusion
  33.2 4.4 collective-permute-done.2
  39.8 14.7 %while.20 = (s32[]{:T(128)}, bf16[2,512,128]{2,1,0:T(8,128)(2,1)S(1)}, s32[2048]{0:T(1024)S(1)}, s32[2]{0:T(128)S(1)}, s32[1024]{0:T(1024)S(1)}, /*index=5*/s32[...) while((s32[]{:T(128)}, ...), condition=%wide.region_3.4_spmd, body=%wide.region_0.3_spmd.sunk | while | flops 558956032 | bytes 16068835 | solution.py:73
  41.0 2.4 select_reduce_fusion.4
  45.2 2.0 fusion.67
  48.4 2.4 select_reduce_fusion.4
  52.6 2.0 fusion.67
  54.6 14.8 %while.21 = (s32[]{:T(128)}, bf16[2,512,128]{2,1,0:T(8,128)(2,1)S(1)}, s32[2048]{0:T(1024)S(1)}, s32[2]{0:T(128)S(1)}, s32[1024]{0:T(1024)S(1)}, /*index=5*/s32[...) while((s32[]{:T(128)}, ...), condition=%wide.region_7.8_spmd, body=%wide.region_4.7_spmd.sunk | while | flops 558956032 | bytes 16068835 | solution.py:73
  55.9 2.4 select_reduce_fusion.5
  60.0 2.0 fusion.71
  63.3 2.4 select_reduce_fusion.5
  67.4 2.0 fusion.71
  69.4 2.4 convolution_convert_fusion.2
  72.2 1.8 reduce-window.6
  75.2 116.7 %reduce-scatter.2.cloned.1.call-done = bf16[128,1280]{1,0:T(8,128)(2,1)} async-done(((bf16[1024,1280]{1,0:T(8,128)(2,1)}), bf16[128,1280]{1,0:T(8,128)(2,1)}) %reduce-scatter.2.cloned.1.call-update) | async-done | bytes 327696 | tf_op jit(solution)/shard_map/reduce_scatter | solution.py:77
  193.1 3.4 convolution_convert_fusion.1
  197.8 16.2 %all-to-all-start = ((bf16[64,16,1280]{2,1,0:T(8,128)(2,1)}), bf16[64,16,1280]{2,1,0:T(8,128)(2,1)S(1)}, u32[]{:S(2)}, u32[]{:S(2)}) async-start(bf16[64,16,1280]{2,1,0:T(8,128)(2,1)} %bitcast.7), calls=%async_computation.1 | async-start | bytes 5242880 | tf_op jit(solution)/shard_map/all_to_all | solution.py:105
  214.8 113.5 %all-gather.2.cloned.1.call-done = bf16[1,768,1280]{2,1,0:T(8,128)(2,1)} async-done(((bf16[1,96,1280]{2,1,0:T(8,128)(2,1)}), bf16[1,768,1280]{2,1,0:T(8,128)(2,1)}) %all-gather.2.cloned.1.call-update) | async-done | bytes 1966096 | tf_op jit(solution)/shard_map/all_gather | solution.py:43
  328.3 19.3 %all-to-all-done = bf16[64,16,1280]{2,1,0:T(8,128)(2,1)S(1)} async-done(((bf16[64,16,1280]{2,1,0:T(8,128)(2,1)}), bf16[64,16,1280]{2,1,0:T(8,128)(2,1)S(1)}, u32[]{:S(2)}, u32[]{:S(2)}) %all-to-all-start) | async-done | bytes 2621472 | tf_op jit(solution)/shard_map/all_to_all | solution.py:105
  347.6 8.0 %convolution_convert_fusion = bf16[1024,1280]{1,0:T(8,128)(2,1)} fusion(bf16[1,768,1280]{2,1,0:T(8,128)(2,1)} %all-gather.2.cloned.1.call-done, bf16[1024,1280]{1,0:T(8,128)(2,1)S(1)} %bitcast.66, bf16[768,1280]{1,0:T(8,128)(2,1)} %bitcast.68), kind=kOutput, calls=%fused_computation.32 | convolution fusion | flops 4031774720 | bytes 9175040 | tf_op jit(solution)/shard_map/dot_general | solution.py:111
  355.6 14.9 %all-to-all-start.2 = ((bf16[64,16,1280]{2,1,0:T(8,128)(2,1)}), bf16[64,16,1280]{2,1,0:T(8,128)(2,1)S(1)}, u32[]{:S(2)}, u32[]{:S(2)}) async-start(bf16[64,16,1280]{2,1,0:T(8,128)(2,1)} %bitcast.67), calls=%async_computation.3 | async-start | bytes 5242880 | tf_op jit(solution)/shard_map/all_to_all | solution.py:113
  370.9 123.9 %all-to-all-done.2 = bf16[64,16,1280]{2,1,0:T(8,128)(2,1)S(1)} async-done(((bf16[64,16,1280]{2,1,0:T(8,128)(2,1)}), bf16[64,16,1280]{2,1,0:T(8,128)(2,1)S(1)}, u32[]{:S(2)}, u32[]{:S(2)}) %all-to-all-start.2) | async-done | bytes 2621472 | tf_op jit(solution)/shard_map/all_to_all | solution.py:113
  494.8 3.7 gather_fusion
  498.5 4.5 reshape.115
  503.0 4.2 multiply_reduce_fusion
  (80 shorter events, 20.5 us)
Async XLA Ops:
  6.5 62.9 %copy-start = (bf16[256,1280]{1,0:T(8,128)(2,1)S(1)}, bf16[256,1280]{1,0:T(8,128)(2,1)}, u32[]{:S(2)}) copy-start(bf16[256,1280]{1,0:T(8,128)(2,1)} %param.19) | copy-start | bytes 1966084
  7.3 22.8 %collective-permute-start = (s32[1024]{0:T(1024)S(1)}, s32[1024]{0:T(1024)S(1)}, u32[]{:S(2)}, u32[]{:S(2)}) collective-permute-start(s32[1024]{0:T(1024)S(1)} %broadcast_add_fusion), channel_id=1, source_target_pairs={{0,8},{8,16},{16,24},{24,32},{32,40},{40,48},{48,56},{56,64},{64,7... | collective-permute-start | bytes 12296 | tf_op jit(solution)/shard_map/ppermute | solution.py:13
  10.8 19.4 %collective-permute-start.1 = (bf16[1024,256]{1,0:T(8,128)(2,1)}, bf16[1024,256]{1,0:T(8,128)(2,1)}, u32[]{:S(2)}, u32[]{:S(2)}) collective-permute-start(bf16[1024,256]{1,0:T(8,128)(2,1)} %param.16), channel_id=1, source_target_pairs={{0,8},{8,16},{16,24},{24,32},{32,40},{40,48},{48,56},{56,64},{64,7... | collective-permute-start | bytes 1572872 | tf_op jit(solution)/shard_map/ppermute | solution.py:13
  14.0 23.6 %collective-permute-start.2 = (bf16[1024,256]{1,0:T(8,128)(2,1)}, bf16[1024,256]{1,0:T(8,128)(2,1)}, u32[]{:S(2)}, u32[]{:S(2)}) collective-permute-start(bf16[1024,256]{1,0:T(8,128)(2,1)} %param.17), channel_id=1, source_target_pairs={{0,8},{8,16},{16,24},{24,32},{32,40},{40,48},{48,56},{56,64},{64,7... | collective-permute-start | bytes 1572872 | tf_op jit(solution)/shard_map/ppermute | solution.py:13
  19.4 177.1 %all-to-all-start.1 = ((bf16[8,1,96,1280]{3,2,1,0:T(8,128)(2,1)}), bf16[8,1,96,1280]{3,2,1,0:T(8,128)(2,1)S(1)}, u32[]{:S(2)}, u32[]{:S(2)}) async-start(bf16[8,1,96,1280]{3,2,1,0:T(8,128)(2,1)} %stack.2), calls=%async_computation.2 | async-start | bytes 3932160 | tf_op jit(solution)/shard_map/all_to_all | solution.py:41
  25.4 166.5 %reduce-scatter.2.cloned.1.call-start = ((), (), s32[]{:S(2)}) async-start(), calls=%async_computation.4 | async-start | bytes 2949120 | tf_op jit(solution)/shard_map/reduce_scatter | solution.py:77
  39.8 14.8 %copy-start.7 = (bf16[1024,128]{1,0:T(8,128)(2,1)S(1)}, bf16[1024,128]{1,0:T(8,128)(2,1)}, u32[]{:S(2)}) copy-start(bf16[1024,128]{1,0:T(8,128)(2,1)} %get-tuple-element.281) | copy-start | bytes 786436
  41.0 4.1 copy-start.6
  48.4 4.1 copy-start.6
  55.9 4.1 copy-start.5
  63.3 4.1 copy-start.5
  69.4 2.4 copy-start.9
  69.4 122.5 %copy-start.1 = (bf16[128,1280]{1,0:T(8,128)(2,1)S(1)}, bf16[128,1280]{1,0:T(8,128)(2,1)}, u32[]{:S(2)}) copy-start(bf16[128,1280]{1,0:T(8,128)(2,1)} %param.20) | copy-start | bytes 983044
  69.4 123.6 %copy-start.8 = (f32[1280]{0:T(1024)S(1)}, f32[1280]{0:T(1024)}, u32[]{:S(2)}) copy-start(f32[1280]{0:T(1024)} %param.21) | copy-start | bytes 15364
  196.5 1.3 copy-start.4
  197.8 149.8 %all-to-all-start = ((bf16[64,16,1280]{2,1,0:T(8,128)(2,1)}), bf16[64,16,1280]{2,1,0:T(8,128)(2,1)S(1)}, u32[]{:S(2)}, u32[]{:S(2)}) async-start(bf16[64,16,1280]{2,1,0:T(8,128)(2,1)} %bitcast.7), calls=%async_computation.1 | async-start | bytes 5242880 | tf_op jit(solution)/shard_map/all_to_all | solution.py:105
  214.0 114.2 %all-gather.2.cloned.1.call-start = ((), (), s32[]{:S(2)}) async-start(), calls=%async_computation.5 | async-start | bytes 2211840 | tf_op jit(solution)/shard_map/all_gather | solution.py:43
  355.6 15.1 %copy-start.10 = (f32[128,6]{0,1:T(8,128)S(1)}, f32[128,6]{0,1:T(8,128)}, u32[]{:S(2)}) copy-start(f32[128,6]{0,1:T(8,128)} %param.23) | copy-start | bytes 9220
  355.6 139.1 %all-to-all-start.2 = ((bf16[64,16,1280]{2,1,0:T(8,128)(2,1)}), bf16[64,16,1280]{2,1,0:T(8,128)(2,1)S(1)}, u32[]{:S(2)}, u32[]{:S(2)}) async-start(bf16[64,16,1280]{2,1,0:T(8,128)(2,1)} %bitcast.67), calls=%async_computation.3 | async-start | bytes 5242880 | tf_op jit(solution)/shard_map/all_to_all | solution.py:113
  503.0 4.2 copy-start.2
  503.0 4.2 copy-start.3
Sparse Core Ops, SparseCore 0:
  71.9 119.9 reduce-scatter.1
  216.9 111.3 all-gather.1
